TPU v7x, 32 devices: a whole 2x2x4 slice. The times are simulated.
32 devices in a mesh: band: 4 (over y, x), patch: 8 (over z, core).
Axes of the slice: x: 2, y: 2, z: 4, core: 2. Of those that a mesh axis runs over, the one named last changes fastest.
Arguments:
- emissivity: float32 [32, 65536], P('band', 'patch'), may hold values from 0.1 to 0.9
- blackbody: float32 [32, 65536], P('band', 'patch'), may hold values from 0.2 to 2
- loss_weights: float32 [32, 65536], P('band', 'patch'), may hold values from 0.5 to 1.5
- view_blocks: bfloat16 [8, 4, 8, 16, 256, 256], P('patch', 'band'), may hold values from 0 to 0.012207031
- column_blocks: int32 [8, 4, 8, 16], P('patch', 'band'), may hold values from 0 to 255, as said below
- patch_owner: int32 [8, 4, 2048, 1], P('patch', 'band'), may hold values from 0 to 31; in each aligned block of 2048 rows (0 to 2047, 2048 to 4095, ..., all dimensions but the last counted through in order) at most 192 rows name the same one
- patch_surface: int32 [8, 4, 2048], P('patch', 'band'), may hold values from 0 to 1023
Outputs:
- radiosity: float32 [32, 8, 4, 2048], P(None, 'patch', 'band')
- surface_grad: float32 [32, 32768], P(None, ('band', 'patch'))
Inputs may be any that keep to these rules, and one draw needn't show every extreme that they name: column_blocks[g, s, r] lists 16 different row-block indices, all among the 96 row blocks of patch groups g - 1, g and g + 1, wrapping around the 8 groups. `patch_owner`: among the 2048 patches of one row-block range no owner is named more than 192 times.
All inputs are finite; a program needn't handle non-finite values.
Results may differ from a plain program's by a relative error of at most 0.0005.
Values may be sent and summed in bfloat16 or wider, within the bound.
No kernel may reach another device: no remote copies, remote signals or barrier semaphores. Data moves between devices by JAX's collectives and lax.ppermute only.
A program may use at most 128 MiB of HBM per device.

v0:
```python
import jax
import jax.numpy as jnp
from jax import lax
from jax.sharding import PartitionSpec as P


def passed_along(block, axis, distance):
    devices = range(lax.axis_size(axis))
    route = [((i - distance) % len(devices), i) for i in devices]
    return lax.ppermute(block, axis, route)


def body(
    emissivity, blackbody, loss_weights, view_blocks, column_blocks, patch_owner, patch_surface
):
    emissive, planck, weighting = (
        lax.all_to_all(emissivity, "band", split_axis=1, concat_axis=0, tiled=True),
        lax.all_to_all(blackbody, "band", split_axis=1, concat_axis=0, tiled=True),
        lax.all_to_all(loss_weights, "band", split_axis=1, concat_axis=0, tiled=True),
    )
    band_count = emissive.shape[0]
    patch_rows = emissive.shape[1]
    rb_count = view_blocks.shape[2]
    depth = view_blocks.shape[3]
    width = view_blocks.shape[4]
    split_count = lax.axis_size("band")
    group_count = lax.axis_size("patch")
    per_group = split_count * rb_count
    block_total = group_count * per_group
    window_start = (lax.axis_index("patch") - 1) * per_group
    offsets = jnp.mod(column_blocks.reshape(rb_count, depth) - window_start, block_total)
    flat_offsets = offsets.reshape(rb_count * depth)
    matrix = view_blocks.reshape(rb_count, depth, width, width)
    emission = emissive * planck
    reflect = 1.0 - emissive

    def window(vector):
        gathered = lax.all_gather(vector, "band", axis=1, tiled=True)
        lower_rows = passed_along(gathered, "patch", 1)
        upper_rows = passed_along(gathered, "patch", -1)
        joined = jnp.concatenate([lower_rows, gathered, upper_rows], axis=1)
        return joined.reshape(band_count, 3 * per_group, width)

    def forward(vector):
        blocks = window(vector)
        picked = blocks[:, offsets]
        result = jnp.einsum("rkij,brkj->bri", matrix, picked, preferred_element_type=jnp.float32)
        return result.reshape(band_count, patch_rows)

    def adjoint(vector):
        partial_terms = jnp.einsum(
            "rkij,bri->brkj",
            matrix,
            vector.reshape(band_count, rb_count, width),
            preferred_element_type=jnp.float32,
        )
        empty = jnp.zeros((band_count, 3 * per_group, width), jnp.float32)
        totals = empty.at[:, flat_offsets].add(
            partial_terms.reshape(band_count, rb_count * depth, width)
        )
        totals = totals.reshape(band_count, 3, split_count, patch_rows)
        from_upper = passed_along(totals[:, 0].astype(jnp.bfloat16), "patch", -1).astype(
            jnp.float32
        )
        from_lower = passed_along(totals[:, 2], "patch", 1)
        combined = totals[:, 1] + from_upper + from_lower
        return lax.psum_scatter(combined, "band", scatter_dimension=1, tiled=True).reshape(
            band_count, patch_rows
        )

    incident_zero = forward(emission.astype(jnp.bfloat16))
    rad_one = emission + reflect * incident_zero
    incident_one = forward(rad_one.astype(jnp.bfloat16))
    radiosity = emission + reflect * incident_one
    adjoint_one = adjoint((reflect * weighting).astype(jnp.bfloat16))
    adjoint_zero = adjoint((reflect * adjoint_one).astype(jnp.bfloat16))
    gradient = (weighting + adjoint_one + adjoint_zero) * planck - (
        weighting * incident_one + adjoint_one * incident_zero
    )
    device_count = split_count * group_count
    capacity = max(2, 3 * patch_rows // device_count)
    surface_count = patch_rows // 2
    owners = patch_owner.reshape(patch_rows)
    locals_index = patch_surface.reshape(patch_rows)
    owner_hits = (owners[:, None] == jnp.arange(device_count, dtype=jnp.int32)[None, :]).astype(
        jnp.int32
    )
    running = jnp.cumsum(owner_hits, axis=0)
    slot_index = jnp.sum(running * owner_hits, axis=1) - 1
    send_values = (
        jnp.zeros((band_count, device_count, capacity), jnp.float32)
        .at[:, owners, slot_index]
        .set(gradient)
    )
    send_labels = (
        jnp.full((1, device_count, capacity), surface_count, jnp.int32)
        .at[0, owners, slot_index]
        .set(locals_index)
    )
    got_values, got_labels = (
        lax.all_to_all(send_values, ("band", "patch"), split_axis=1, concat_axis=1, tiled=True),
        lax.all_to_all(send_labels, ("band", "patch"), split_axis=1, concat_axis=1, tiled=True),
    )
    flat_values = got_values.reshape(band_count, device_count * capacity)
    flat_labels = got_labels.reshape(device_count * capacity)
    surface_sums = jax.ops.segment_sum(flat_values.T, flat_labels, surface_count + 1)[
        :surface_count
    ].T
    surface_counts = jax.ops.segment_sum(
        jnp.ones((device_count * capacity,), jnp.float32), flat_labels, surface_count + 1
    )[:surface_count]
    surface_grad = surface_sums / jnp.maximum(surface_counts, 1.0)[None, :]
    return (radiosity.reshape(band_count, 1, 1, patch_rows), surface_grad)


def solution(mesh):
    in_specs = (
        P("band", "patch"),
        P("band", "patch"),
        P("band", "patch"),
        P("patch", "band", None, None, None, None),
        P("patch", "band", None, None),
        P("patch", "band", None, None),
        P("patch", "band", None),
    )
    out_specs = (P(None, "patch", "band", None), P(None, ("band", "patch")))
    return jax.shard_map(body, mesh=mesh, in_specs=in_specs, out_specs=out_specs, check_vma=False)
```

profile of v0, /device:TPU:1, one launch (start us, length us, event | category | flops | bytes accessed | tf_op | source)
XLA Modules:
  0.0 336.8 jit_solution(3225798159353689433)
XLA Ops:
  7.2 4.3 %all-to-all-start = ((f32[8,4,2048]{2,0,1:T(8,128)}), f32[8,4,2048]{2,0,1:T(8,128)S(1)}, u32[]{:S(2)}, u32[]{:S(2)}) async-start(f32[8,4,2048]{2,0,1:T(8,128)} %bitcast.215), calls=%async_computation | async-start | bytes 524288 | tf_op jit(solution)/shard_map/all_to_all | solution.py:17
  12.3 0.7 fusion.35
  13.1 9.1 %reduce-window.6 = s32[32,16,128]{2,1,0:T(8,128)S(1)} reduce-window(s32[32,16,128]{2,1,0:T(8,128)S(1)} %fusion.35, s32[]{:T(128)} %constant.21.clone.1), window={size=1x1x128 pad=0_0x0_0x127_0}, to_apply=%region_0.1 | reduce-window | flops 8323072 | bytes 524292 | tf_op jit(solution)/shard_map/reduce-window
  22.9 0.8 fusion.23
  23.7 0.7 compare_select_fusion
  24.4 0.7 multiply_reduce_fusion.1
  25.1 0.8 and_reduce_fusion
  26.1 8.2 %scatter_custom_fusion.4 = s32[6144]{0:T(1024)S(1)} fusion(s32[2048]{0:T(1024)S(1)} %broadcast_select_fusion.1, s32[2048]{0:T(1024)} %bitcast.222, s32[]{:T(128)} %constant.29.clone.1), kind=kCustom, calls=%fused_computation.78 | custom fusion | bytes 25088
  34.4 0.7 reshape.309
  35.1 3.6 %all-to-all-start.3 = ((f32[8,4,2048]{2,0,1:T(8,128)}), f32[8,4,2048]{2,0,1:T(8,128)S(1)}, u32[]{:S(2)}, u32[]{:S(2)}) async-start(f32[8,4,2048]{2,0,1:T(8,128)} %bitcast.30), calls=%async_computation.3 | async-start | bytes 524288 | tf_op jit(solution)/shard_map/all_to_all | solution.py:19
  38.9 4.1 %all-to-all-done.3 = f32[8,4,2048]{2,0,1:T(8,128)S(1)} async-done(((f32[8,4,2048]{2,0,1:T(8,128)}), f32[8,4,2048]{2,0,1:T(8,128)S(1)}, u32[]{:S(2)}, u32[]{:S(2)}) %all-to-all-start.3) | async-done | bytes 262176 | tf_op jit(solution)/shard_map/all_to_all | solution.py:19
  43.0 4.1 %all-to-all-start.1 = ((f32[8,4,2048]{2,0,1:T(8,128)}), f32[8,4,2048]{2,0,1:T(8,128)}, u32[]{:S(2)}, u32[]{:S(2)}) async-start(f32[8,4,2048]{2,0,1:T(8,128)} %bitcast.2), calls=%async_computation.1 | async-start | bytes 524288 | tf_op jit(solution)/shard_map/all_to_all | solution.py:18
  47.2 10.6 %fusion.2 = f32[8,32,16,256]{3,1,2,0:T(8,128)} fusion(bf16[1,1,8,16,256,256]{5,4,3,2,1,0:T(8,128)(2,1)} %param.10, bf16[32,8,256,1]{2,1,0,3:T(8,128)(2,1)S(1)} %bitcast.214), kind=kOutput, calls=%fused_computation.10 | convolution fusion | flops 536870912 | bytes 21102592 | tf_op jit(solution)/shard_map/rkij,bri->brkj/dot_general | solution.py:51
  58.2 13.5 %scatter_fusion = f32[32,96,256]{2,0,1:T(8,128)S(1)} fusion(f32[32,96,256]{2,0,1:T(8,128)S(1)} %broadcast.223.clone, s32[128]{0:T(128)S(1)} %fusion.45, f32[128,32,256]{2,1,0:T(8,128)} %bitcast.195), kind=kCustom, calls=%fused_computation.2 | custom fusion | flops 1048576 | bytes 12583424 | tf_op jit(solution)/shard_map/scatter-add | solution.py:58
  71.7 3.5 %copy.102 = f32[32,96,256]{2,1,0:T(8,128)} copy(f32[32,96,256]{2,0,1:T(8,128)S(1)} %scatter_fusion) | data formatting | bytes 6291456 | tf_op jit(solution)/shard_map/scatter-add | solution.py:58
  75.1 3.4 %reshape.298 = f32[32,3,4,2048]{3,2,1,0:T(4,128)S(1)} reshape(f32[32,96,256]{2,1,0:T(8,128)} %copy.102) | data formatting | bytes 6291456 | tf_op jit(solution)/shard_map/reshape | solution.py:61
  78.6 1.5 fusion.47
  80.1 3.8 %collective-permute-start.5 = (f32[32,4,2048]{2,1,0:T(4,128)}, f32[32,4,2048]{2,1,0:T(4,128)}, u32[]{:S(2)}, u32[]{:S(2)}) collective-permute-start(f32[32,4,2048]{2,1,0:T(4,128)} %get-tuple-element.19), channel_id=1, source_target_pairs={{7,0},{0,1},{1,2},{2,3},{3,4},{4,5},{5,6},{6,7},{15,8},{8,9},{9,10... | collective-permute-start | bytes 3145736 | tf_op jit(solution)/shard_map/ppermute | solution.py:10
  83.9 1.0 fusion.17
  84.9 6.6 %all-to-all-start.2 = ((s32[1,32,192]{2,0,1:T(1,128)}), s32[1,32,192]{2,0,1:T(1,128)S(1)}, u32[]{:S(2)}, u32[]{:S(2)}) async-start(s32[1,32,192]{2,0,1:T(1,128)} %reshape.309), calls=%async_computation.2 | async-start | bytes 65536 | tf_op jit(solution)/shard_map/all_to_all | solution.py:102
  91.6 1.0 fusion.38
  92.5 9.1 %all_gather.6 = bf16[32,8192]{1,0:T(8,128)(2,1)S(1)} all-gather(bf16[32,2048]{1,0:T(8,128)(2,1)S(1)} %fusion.38), channel_id=1, replica_groups=mesh['band'=4,'patch'=8] {'band'}, dimensions={1}, use_global_device_ids=true | all-gather | bytes 655360 | tf_op jit(solution)/shard_map/all_gather | solution.py:38
  101.6 2.8 collective-permute-start
  104.4 2.0 fusion.16
  106.4 1.6 copy.105
  108.2 5.3 %collective-permute-done = bf16[32,8192]{1,0:T(8,128)(2,1)S(1)} collective-permute-done((bf16[32,8192]{1,0:T(8,128)(2,1)S(1)}, bf16[32,8192]{1,0:T(8,128)(2,1)S(1)}, u32[]{:S(2)}, u32[]{:S(2)}) %collective-permute-start) | collective-permute-done | bytes 524320 | tf_op jit(solution)/shard_map/ppermute | solution.py:10
  113.5 5.5 %collective-permute-done.1 = bf16[32,8192]{1,0:T(8,128)(2,1)S(1)} collective-permute-done((bf16[32,8192]{1,0:T(8,128)(2,1)S(1)}, bf16[32,8192]{1,0:T(8,128)(2,1)S(1)}, u32[]{:S(2)}, u32[]{:S(2)}) %collective-permute-start.1) | collective-permute-done | bytes 524320 | tf_op jit(solution)/shard_map/ppermute | solution.py:10
  119.1 1.4 copy.163
  120.4 2.1 gather_fusion
  122.6 10.8 %fusion.10 = f32[8,4,8,256]{3,2,1,0:T(8,128)S(1)} fusion(bf16[32,8,16,256]{3,0,2,1:T(8,128)(2,1)S(1)} %bitcast.198, bf16[1,1,8,16,256,256]{5,4,3,2,1,0:T(8,128)(2,1)} %param.10), kind=kOutput, calls=%fused_computation.22 | convolution fusion | flops 536870912 | bytes 19136512 | tf_op jit(solution)/shard_map/rkij,brkj->bri/dot_general | solution.py:47
  133.4 0.7 copy.133
  134.1 1.7 reduce-scatter.7.cloned.1.call-done
  135.9 1.0 copy.137
  137.0 10.6 %fusion = f32[8,32,16,256]{3,1,2,0:T(8,128)} fusion(bf16[1,1,8,16,256,256]{5,4,3,2,1,0:T(8,128)(2,1)} %param.10, bf16[32,8,256,1]{2,1,0,3:T(8,128)(2,1)S(1)} %bitcast.213), kind=kOutput, calls=%fused_computation.8 | convolution fusion | flops 536870912 | bytes 21102592 | tf_op jit(solution)/shard_map/rkij,bri->brkj/dot_general | solution.py:51
  147.9 13.5 %scatter_fusion.1 = f32[32,96,256]{2,0,1:T(8,128)S(1)} fusion(f32[32,96,256]{2,0,1:T(8,128)S(1)} %broadcast.223, s32[128]{0:T(128)S(1)} %fusion.45, f32[128,32,256]{2,1,0:T(8,128)} %bitcast.194), kind=kCustom, calls=%fused_computation.3 | custom fusion | flops 1048576 | bytes 12583424 | tf_op jit(solution)/shard_map/scatter-add | solution.py:58
  161.4 3.5 %copy.107 = f32[32,96,256]{2,1,0:T(8,128)} copy(f32[32,96,256]{2,0,1:T(8,128)S(1)} %scatter_fusion.1) | data formatting | bytes 6291456 | tf_op jit(solution)/shard_map/scatter-add | solution.py:58
  164.9 3.4 %reshape.302 = f32[32,3,4,2048]{3,2,1,0:T(4,128)S(1)} reshape(f32[32,96,256]{2,1,0:T(8,128)} %copy.107) | data formatting | bytes 6291456 | tf_op jit(solution)/shard_map/reshape | solution.py:61
  168.5 1.8 collective-permute-start.7
  170.6 1.0 fusion.33
  171.6 9.0 %all_gather.7 = bf16[32,8192]{1,0:T(8,128)(2,1)S(1)} all-gather(bf16[32,2048]{1,0:T(8,128)(2,1)S(1)} %fusion.33), channel_id=1, replica_groups=mesh['band'=4,'patch'=8] {'band'}, dimensions={1}, use_global_device_ids=true | all-gather | bytes 655360 | tf_op jit(solution)/shard_map/all_gather | solution.py:38
  180.7 2.6 collective-permute-start.2
  183.3 1.6 collective-permute-start.3
  184.9 2.1 collective-permute-done.6
  188.1 1.6 copy.110
  189.7 7.9 %collective-permute-done.2 = bf16[32,8192]{1,0:T(8,128)(2,1)S(1)} collective-permute-done((bf16[32,8192]{1,0:T(8,128)(2,1)S(1)}, bf16[32,8192]{1,0:T(8,128)(2,1)S(1)}, u32[]{:S(2)}, u32[]{:S(2)}) %collective-permute-start.2) | collective-permute-done | bytes 524320 | tf_op jit(solution)/shard_map/ppermute | solution.py:10
  197.6 2.6 collective-permute-done.3
  200.4 1.4 copy.162
  201.7 2.1 gather_fusion.1
  203.9 11.0 %fusion.4 = f32[8,32,256,1]{2,1,3,0:T(8,128)S(1)} fusion(bf16[32,8,16,256]{3,0,2,1:T(8,128)(2,1)S(1)} %bitcast.197, bf16[1,1,8,16,256,256]{5,4,3,2,1,0:T(8,128)(2,1)} %param.10), kind=kOutput, calls=%fused_computation.12 | convolution fusion | flops 536870912 | bytes 19136512 | tf_op jit(solution)/shard_map/rkij,brkj->bri/dot_general | solution.py:47
  214.9 5.2 %reduce-scatter.9.cloned.1.call-done = f32[32,1,2048]{2,0,1:T(8,128)} async-done(((f32[32,4,2048]{2,0,1:T(8,128)}), f32[32,1,2048]{2,0,1:T(8,128)}) %reduce-scatter.9.cloned.1.call-update) | async-done | bytes 262160
  220.1 1.2 fusion.29
  221.3 1.3 copy.112
  222.7 6.7 %scatter_custom_fusion.5 = f32[32,6144]{0,1:T(8,128)S(1)} fusion(s32[2048]{0:T(1024)S(1)} %broadcast_select_fusion, f32[2048,32]{1,0:T(8,128)} %copy.112, f32[]{:T(128)} %constant.25.clone.1), kind=kCustom, calls=%fused_computation.20 | custom fusion | bytes 786944
  229.4 2.2 copy.113
  231.6 5.1 %all-to-all-start.4 = ((f32[32,32,192]{2,0,1:T(8,128)}), f32[32,32,192]{2,0,1:T(8,128)S(1)}, u32[]{:S(2)}, u32[]{:S(2)}) async-start(f32[32,32,192]{2,0,1:T(8,128)} %copy.113), calls=%async_computation.4 | async-start | bytes 2097152 | tf_op jit(solution)/shard_map/all_to_all | solution.py:101
  236.9 42.6 %scatter_custom_fusion.3 = f32[1025]{0:T(1024)S(1)} fusion(s32[6144]{0:T(1024)S(1)} %reshape.348, f32[6144]{0:T(1024)S(1)} %broadcast.242, f32[]{:T(128)} %constant.25.clone.1), kind=kCustom, calls=%fused_computation.87 | custom fusion | flops 6144 | bytes 4104 | tf_op jit(solution)/shard_map/scatter-add | solution.py:109
  279.5 1.1 copy.98
  280.7 1.0 fusion.34
  281.7 1.0 copy.116
  283.3 1.3 reshape.305
  284.5 2.0 copy.115
  286.5 41.4 %scatter_custom_fusion.2 = f32[1025,32]{1,0:T(8,128)} fusion(s32[6144]{0:T(1024)S(1)} %reshape.348, f32[6144,32]{1,0:T(8,128)S(1)} %copy.115, f32[]{:T(128)} %constant.25.clone.1), kind=kCustom, calls=%fused_computation.37 | custom fusion | flops 196608 | bytes 131204 | tf_op jit(solution)/shard_map/scatter-add | solution.py:106
  327.9 1.2 fusion.19
  329.2 0.8 copy.117
  (66 shorter events, 5.8 us)
Async XLA Ops:
  7.2 18.8 %copy-start.7 = (s32[3]{0:T(128)S(1)}, s32[3]{0:T(128)}, u32[]{:S(2)}) copy-start(s32[3]{0:T(128)} %constant.59) | copy-start | bytes 40
  7.2 18.9 %copy-start.8 = (s32[3]{0:T(128)S(1)}, s32[3]{0:T(128)}, u32[]{:S(2)}) copy-start(s32[3]{0:T(128)} %constant.62) | copy-start | bytes 40
  7.2 27.9 %all-to-all-start = ((f32[8,4,2048]{2,0,1:T(8,128)}), f32[8,4,2048]{2,0,1:T(8,128)S(1)}, u32[]{:S(2)}, u32[]{:S(2)}) async-start(f32[8,4,2048]{2,0,1:T(8,128)} %bitcast.215), calls=%async_computation | async-start | bytes 524288 | tf_op jit(solution)/shard_map/all_to_all | solution.py:17
  35.1 7.9 %all-to-all-start.3 = ((f32[8,4,2048]{2,0,1:T(8,128)}), f32[8,4,2048]{2,0,1:T(8,128)S(1)}, u32[]{:S(2)}, u32[]{:S(2)}) async-start(f32[8,4,2048]{2,0,1:T(8,128)} %bitcast.30), calls=%async_computation.3 | async-start | bytes 524288 | tf_op jit(solution)/shard_map/all_to_all | solution.py:19
  38.9 18.9 %copy-start.5 = (f32[4,8,8,256]{3,2,1,0:T(8,128)}, f32[4,8,8,256]{3,2,1,0:T(8,128)S(1)}, u32[]{:S(2)}) copy-start(f32[4,8,8,256]{3,2,1,0:T(8,128)S(1)} %copy.135) | copy-start | bytes 786436
  43.0 14.8 %copy-start.3 = (f32[8,4,2048]{2,0,1:T(8,128)}, f32[8,4,2048]{2,0,1:T(8,128)S(1)}, u32[]{:S(2)}) copy-start(f32[8,4,2048]{2,0,1:T(8,128)S(1)} %all-to-all-done.3) | copy-start | bytes 786436
  43.0 41.9 %all-to-all-start.1 = ((f32[8,4,2048]{2,0,1:T(8,128)}), f32[8,4,2048]{2,0,1:T(8,128)}, u32[]{:S(2)}, u32[]{:S(2)}) async-start(f32[8,4,2048]{2,0,1:T(8,128)} %bitcast.2), calls=%async_computation.1 | async-start | bytes 524288 | tf_op jit(solution)/shard_map/all_to_all | solution.py:18
  80.1 24.3 %collective-permute-start.5 = (f32[32,4,2048]{2,1,0:T(4,128)}, f32[32,4,2048]{2,1,0:T(4,128)}, u32[]{:S(2)}, u32[]{:S(2)}) collective-permute-start(f32[32,4,2048]{2,1,0:T(4,128)} %get-tuple-element.19), channel_id=1, source_target_pairs={{7,0},{0,1},{1,2},{2,3},{3,4},{4,5},{5,6},{6,7},{15,8},{8,9},{9,10... | collective-permute-start | bytes 3145736 | tf_op jit(solution)/shard_map/ppermute | solution.py:10
  84.9 19.5 %collective-permute-start.4 = (bf16[32,4,2048]{2,1,0:T(4,128)(2,1)}, bf16[32,4,2048]{2,1,0:T(4,128)(2,1)S(1)}, u32[]{:S(2)}, u32[]{:S(2)}) collective-permute-start(bf16[32,4,2048]{2,1,0:T(4,128)(2,1)} %fusion.17), channel_id=1, source_target_pairs={{1,0},{2,1},{3,2},{4,3},{5,4},{6,5},{7,6},{0,7},{9,8},{10,9},{11,1... | collective-permute-start | bytes 1572872 | tf_op jit(solution)/shard_map/ppermute | solution.py:10
  84.9 146.7 %all-to-all-start.2 = ((s32[1,32,192]{2,0,1:T(1,128)}), s32[1,32,192]{2,0,1:T(1,128)S(1)}, u32[]{:S(2)}, u32[]{:S(2)}) async-start(s32[1,32,192]{2,0,1:T(1,128)} %reshape.309), calls=%async_computation.2 | async-start | bytes 65536 | tf_op jit(solution)/shard_map/all_to_all | solution.py:102
  91.5 44.4 %reduce-scatter.7.cloned.1.call-start = ((), (), s32[]{:S(2)}) async-start(), calls=%async_computation.7 | async-start | bytes 1310720
  101.6 11.9 %collective-permute-start = (bf16[32,8192]{1,0:T(8,128)(2,1)S(1)}, bf16[32,8192]{1,0:T(8,128)(2,1)S(1)}, u32[]{:S(2)}, u32[]{:S(2)}) collective-permute-start(bf16[32,8192]{1,0:T(8,128)(2,1)S(1)} %all_gather.6), channel_id=1, source_target_pairs={{7,0},{0,1},{1,2},{2,3},{3,4},{4,5},{5,6},{6,7},{15,8},{8,9},{9,10... | collective-permute-start | bytes 1572872 | tf_op jit(solution)/shard_map/ppermute | solution.py:10
  104.4 14.6 %collective-permute-start.1 = (bf16[32,8192]{1,0:T(8,128)(2,1)S(1)}, bf16[32,8192]{1,0:T(8,128)(2,1)S(1)}, u32[]{:S(2)}, u32[]{:S(2)}) collective-permute-start(bf16[32,8192]{1,0:T(8,128)(2,1)S(1)} %all_gather.6), channel_id=1, source_target_pairs={{1,0},{2,1},{3,2},{4,3},{5,4},{6,5},{7,6},{0,7},{9,8},{10,9},{11,1... | collective-permute-start | bytes 1572872 | tf_op jit(solution)/shard_map/ppermute | solution.py:10
  108.0 112.1 %reduce-scatter.9.cloned.1.call-start = ((), (), s32[]{:S(2)}) async-start(), calls=%async_computation.8 | async-start | bytes 1310720
  122.6 14.4 %copy-start.6 = (f32[4,8,8,256]{3,2,1,0:T(8,128)S(1)}, f32[4,8,8,256]{3,2,1,0:T(8,128)}, u32[]{:S(2)}) copy-start(f32[4,8,8,256]{3,2,1,0:T(8,128)} %copy-done.5) | copy-start | bytes 786436
  168.3 2.3 copy-start.1
  168.5 19.2 %collective-permute-start.7 = (f32[32,4,2048]{2,1,0:T(4,128)S(1)}, f32[32,4,2048]{2,1,0:T(4,128)S(1)}, u32[]{:S(2)}, u32[]{:S(2)}) collective-permute-start(f32[32,4,2048]{2,1,0:T(4,128)S(1)} %get-tuple-element.17), channel_id=1, source_target_pairs={{7,0},{0,1},{1,2},{2,3},{3,4},{4,5},{5,6},{6,7},{15,8},{8,9},{9,10... | collective-permute-start | bytes 3145736 | tf_op jit(solution)/shard_map/ppermute | solution.py:10
  170.5 16.5 %collective-permute-start.6 = (bf16[32,4,2048]{2,1,0:T(4,128)(2,1)S(1)}, bf16[32,4,2048]{2,1,0:T(4,128)(2,1)S(1)}, u32[]{:S(2)}, u32[]{:S(2)}) collective-permute-start(bf16[32,4,2048]{2,1,0:T(4,128)(2,1)S(1)} %fusion.18), channel_id=1, source_target_pairs={{1,0},{2,1},{3,2},{4,3},{5,4},{6,5},{7,6},{0,7},{9,8},{10,9},{11,1... | collective-permute-start | bytes 1572872 | tf_op jit(solution)/shard_map/ppermute | solution.py:10
  180.7 16.9 %collective-permute-start.2 = (bf16[32,8192]{1,0:T(8,128)(2,1)S(1)}, bf16[32,8192]{1,0:T(8,128)(2,1)S(1)}, u32[]{:S(2)}, u32[]{:S(2)}) collective-permute-start(bf16[32,8192]{1,0:T(8,128)(2,1)S(1)} %all_gather.7), channel_id=1, source_target_pairs={{7,0},{0,1},{1,2},{2,3},{3,4},{4,5},{5,6},{6,7},{15,8},{8,9},{9,10... | collective-permute-start | bytes 1572872 | tf_op jit(solution)/shard_map/ppermute | solution.py:10
  183.3 16.9 %collective-permute-start.3 = (bf16[32,8192]{1,0:T(8,128)(2,1)S(1)}, bf16[32,8192]{1,0:T(8,128)(2,1)S(1)}, u32[]{:S(2)}, u32[]{:S(2)}) collective-permute-start(bf16[32,8192]{1,0:T(8,128)(2,1)S(1)} %all_gather.7), channel_id=1, source_target_pairs={{1,0},{2,1},{3,2},{4,3},{5,4},{6,5},{7,6},{0,7},{9,8},{10,9},{11,1... | collective-permute-start | bytes 1572872 | tf_op jit(solution)/shard_map/ppermute | solution.py:10
  203.9 16.2 %copy-start.2 = (f32[8,4,8,256]{3,2,0,1:T(8,128)S(1)}, f32[8,4,8,256]{3,2,0,1:T(8,128)}, u32[]{:S(2)}) copy-start(f32[8,4,8,256]{3,2,0,1:T(8,128)} %copy.133) | copy-start | bytes 786436
  203.9 16.2 %copy-start.4 = (f32[8,4,2048]{2,0,1:T(8,128)S(1)}, f32[8,4,2048]{2,0,1:T(8,128)}, u32[]{:S(2)}) copy-start(f32[8,4,2048]{2,0,1:T(8,128)} %copy-done.3) | copy-start | bytes 786436
  214.9 6.4 %copy-start = (f32[8,32,256,1]{2,1,3,0:T(8,128)}, f32[8,32,256,1]{2,1,3,0:T(8,128)S(1)}, u32[]{:S(2)}) copy-start(f32[8,32,256,1]{2,1,3,0:T(8,128)S(1)} %fusion.4) | copy-start | bytes 786436
  231.6 51.1 %all-to-all-start.4 = ((f32[32,32,192]{2,0,1:T(8,128)}), f32[32,32,192]{2,0,1:T(8,128)S(1)}, u32[]{:S(2)}, u32[]{:S(2)}) async-start(f32[32,32,192]{2,0,1:T(8,128)} %copy.113), calls=%async_computation.4 | async-start | bytes 2097152 | tf_op jit(solution)/shard_map/all_to_all | solution.py:101
Sparse Core Ops, SparseCore 0:
  108.1 27.7 reduce-scatter.6
  189.9 30.2 reduce-scatter.8
where the time goes:
time: 339 us; the launch traced here: 337 us
  other arithmetic  133 us (39%)
  local copies, waits for them, and re-layouts  56.2 us (17%)
  matrix products  43 us (13%)
  starting transfers between devices  36.7 us (11%)
  waiting for transfers between devices  35.1 us (10%)
  blocking collectives  18.1 us (5%)
  between operations  14.5 us (4%)
    scatter-add x1, other arithmetic, body(): jax.ops.segment_sum(jnp.ones((device_count * capacity,), jnp.float32), fl...  42.6 us
    scatter-add x1, other arithmetic, body(): jax.ops.segment_sum(flat_values.T, flat_labels, surface_count + 1)  41.4 us
    scatter-add x2, other arithmetic, adjoint(): empty.at[:, flat_offsets]  26.9 us
    ppermute x8, waiting for transfers between devices, passed_along(): return lax.ppermute(block, axis, route)  24 us
    dot_general x2, matrix products, forward(): jnp.einsum('rkij,brkj->bri', matrix, picked, preferred_element_type=jnp.f...  21.8 us
    dot_general x2, matrix products, adjoint(): jnp.einsum('rkij,bri->brkj', matrix, vector.reshape(band_count, rb_count,...  21.2 us
    all_gather x2, blocking collectives, window(): gathered = lax.all_gather(vector, 'band', axis=1, tiled=True)  18.1 us
    unnamed x25, local copies, waits for them, and re-layouts  18 us
  transfers between devices with their start and end apart: 15, of which 9 were waited for; matrix products, arithmetic and copies ran while one was open for 55% of the time, Pallas kernels for 0%

commit v1 on v0

--- a/solution.py
+++ b/solution.py
@@ -35,7 +35,37 @@
     reflect = 1.0 - emissive
 
     def window(vector):
-        gathered = lax.all_gather(vector, "band", axis=1, tiled=True)
+
+        def classes_watch(buf):
+            along_axis = "band"
+            known = lax.axis_size(along_axis)
+            z2 = lax.axis_index(along_axis)
+            vec_out, w1, local_next = (known, z2, buf.shape[1])
+            history = []
+            for h, kk in enumerate(buf.shape):
+                history.append(kk * vec_out if h == 1 else kk)
+            taken_in = jnp.zeros(history, buf.dtype)
+            item_now = lax.dynamic_update_slice_in_dim(taken_in, buf, w1 * local_next, axis=1)
+            y2 = value_now = buf
+            for j0 in tuple(range(1, vec_out // 2 + 1)):
+                trail = []
+                for h in [*range(vec_out)]:
+                    trail.append((h, (h + 1) % vec_out))
+                y2 = lax.ppermute(y2, along_axis, trail)
+                item_now = lax.dynamic_update_slice_in_dim(
+                    item_now, y2, (w1 - j0) % vec_out * local_next, axis=1
+                )
+                if 2 * j0 < vec_out:
+                    tray = []
+                    for h in [*range(vec_out)]:
+                        tray.append((h, (h - 1) % vec_out))
+                    value_now = lax.ppermute(value_now, along_axis, tray)
+                    item_now = lax.dynamic_update_slice_in_dim(
+                        item_now, value_now, (w1 + j0) % vec_out * local_next, axis=1
+                    )
+            return item_now
+
+        gathered = classes_watch(vector)
         lower_rows = passed_along(gathered, "patch", 1)
         upper_rows = passed_along(gathered, "patch", -1)
         joined = jnp.concatenate([lower_rows, gathered, upper_rows], axis=1)

time: 339 us -> 353 us (1.041)
  waiting for transfers between devices: 35.1 us -> 54.4 us
  blocking collectives: 18.1 us -> 0 us
  starting transfers between devices: 36.7 us -> 44.3 us
  local copies, waits for them, and re-layouts: 56.2 us -> 62.2 us
    all_gather x2 -> x0, blocking collectives: 18.1 us -> none  [window(): gathered = lax.all_gather(vector, 'band', axis=1, tiled=True)]
    ppermute x8, waiting for transfers between devices: 24 us -> 36.6 us  [passed_along(): return lax.ppermute(block, axis, route)]
    dynamic_update_slice x0 -> x6, local copies, waits for them, and re-layouts: none -> 6.88 us  [the longest x4 3.71 us: classes_watch(): lax.dynamic_update_slice_in_dim(item_now, y2, (w1 - j0) % vec_out * local...]
    ppermute x0 -> x6, starting transfers between devices: none -> 5.98 us  [the longest x4 3.95 us: classes_watch(): y2 = lax.ppermute(y2, along_axis, trail)]
    ppermute x0 -> x6, waiting for transfers between devices: none -> 5.36 us  [the longest x4 5.35 us: classes_watch(): y2 = lax.ppermute(y2, along_axis, trail)]
    all_to_all x1, waiting for transfers between devices: 4.1 us -> 0.12 us  [body(): lax.all_to_all(loss_weights, 'band', split_axis=1, concat_axis=0, tiled=T...]
    all_to_all x1, waiting for transfers between devices: 0.01 us -> 3.68 us  [body(): lax.all_to_all(blackbody, 'band', split_axis=1, concat_axis=0, tiled=True)]
    unnamed x25 -> x41, local copies, waits for them, and re-layouts: 18 us -> 18.3 us
  transfers between devices with their start and end apart: 15 -> 21, of which waited for: 9 -> 11; matrix products, arithmetic and copies ran while one was open for 55% -> 54% of each run, Pallas kernels for 0% -> 0%
where the time goes in v1:
time: 353 us; the launch traced here: 351 us
  other arithmetic  132 us (37%)
  local copies, waits for them, and re-layouts  62.2 us (18%)
  waiting for transfers between devices  54.4 us (15%)
  starting transfers between devices  44.3 us (13%)
  matrix products  43.5 us (12%)
  between operations  14.6 us (4%)
    scatter-add x1, other arithmetic, body(): jax.ops.segment_sum(jnp.ones((device_count * capacity,), jnp.float32), fl...  42.6 us
    scatter-add x1, other arithmetic, body(): jax.ops.segment_sum(flat_values.T, flat_labels, surface_count + 1)  41.4 us
    ppermute x8, waiting for transfers between devices, passed_along(): return lax.ppermute(block, axis, route)  36.6 us
    scatter-add x2, other arithmetic, adjoint(): empty.at[:, flat_offsets]  27 us
    dot_general x2, matrix products, forward(): jnp.einsum('rkij,brkj->bri', matrix, picked, preferred_element_type=jnp.f...  22.2 us
    dot_general x2, matrix products, adjoint(): jnp.einsum('rkij,bri->brkj', matrix, vector.reshape(band_count, rb_count,...  21.2 us
    unnamed x41, local copies, waits for them, and re-layouts  18.3 us
    ppermute x8, starting transfers between devices, passed_along(): return lax.ppermute(block, axis, route)  11.9 us
  transfers between devices with their start and end apart: 21, of which 11 were waited for; matrix products, arithmetic and copies ran while one was open for 54% of the time, Pallas kernels for 0%

profile of v1, /device:TPU:1, one launch (start us, length us, event | category | flops | bytes accessed | tf_op | source)
XLA Modules:
  0.0 351.2 jit_solution(5567197854694126297)
XLA Ops:
  7.2 4.4 %all-to-all-start = ((f32[8,4,2048]{2,0,1:T(8,128)}), f32[8,4,2048]{2,0,1:T(8,128)S(1)}, u32[]{:S(2)}, u32[]{:S(2)}) async-start(f32[8,4,2048]{2,0,1:T(8,128)} %bitcast.219), calls=%async_computation | async-start | bytes 524288 | tf_op jit(solution)/shard_map/all_to_all | solution.py:17
  13.2 9.1 %reduce-window.6 = s32[32,16,128]{2,1,0:T(8,128)S(1)} reduce-window(s32[32,16,128]{2,1,0:T(8,128)S(1)} %fusion.35, s32[]{:T(128)} %constant.79.clone.1), window={size=1x1x128 pad=0_0x0_0x127_0}, to_apply=%region_0.1 | reduce-window | flops 8323072 | bytes 524292 | tf_op jit(solution)/shard_map/reduce-window
  24.2 8.2 %scatter_custom_fusion.4 = s32[6144]{0:T(1024)S(1)} fusion(s32[2048]{0:T(1024)S(1)} %broadcast_select_fusion.1, s32[2048]{0:T(1024)} %bitcast.226, s32[]{:T(128)} %constant.94.clone.1), kind=kCustom, calls=%fused_computation.78 | custom fusion | bytes 25088
  33.3 3.6 %all-to-all-start.1 = ((f32[8,4,2048]{2,0,1:T(8,128)}), f32[8,4,2048]{2,0,1:T(8,128)S(1)}, u32[]{:S(2)}, u32[]{:S(2)}) async-start(f32[8,4,2048]{2,0,1:T(8,128)} %bitcast.2), calls=%async_computation.1 | async-start | bytes 524288 | tf_op jit(solution)/shard_map/all_to_all | solution.py:18
  37.5 3.7 %all-to-all-done.1 = f32[8,4,2048]{2,0,1:T(8,128)S(1)} async-done(((f32[8,4,2048]{2,0,1:T(8,128)}), f32[8,4,2048]{2,0,1:T(8,128)S(1)}, u32[]{:S(2)}, u32[]{:S(2)}) %all-to-all-start.1) | async-done | bytes 262176 | tf_op jit(solution)/shard_map/all_to_all | solution.py:18
  41.2 3.4 all-to-all-start.3
  44.6 0.9 broadcast.223.clone
  46.2 1.4 collective-permute-start
  47.6 0.9 collective-permute-start.1
  48.8 9.7 %all-to-all-start.2 = ((s32[1,32,192]{2,0,1:T(1,128)}), s32[1,32,192]{2,0,1:T(1,128)}, u32[]{:S(2)}, u32[]{:S(2)}) async-start(s32[1,32,192]{2,0,1:T(1,128)} %reshape.309), calls=%async_computation.2 | async-start | bytes 65536 | tf_op jit(solution)/shard_map/all_to_all | solution.py:132
  58.6 10.6 %fusion.2 = f32[8,32,16,256]{3,1,2,0:T(8,128)} fusion(bf16[1,1,8,16,256,256]{5,4,3,2,1,0:T(8,128)(2,1)} %param.10, bf16[32,8,256,1]{2,1,0,3:T(8,128)(2,1)S(1)} %bitcast.218), kind=kOutput, calls=%fused_computation.10 | convolution fusion | flops 536870912 | bytes 21102592 | tf_op jit(solution)/shard_map/rkij,bri->brkj/dot_general | solution.py:81
  69.6 13.6 %scatter_fusion = f32[32,96,256]{2,0,1:T(8,128)S(1)} fusion(f32[32,96,256]{2,0,1:T(8,128)S(1)} %broadcast.230.clone, s32[128]{0:T(128)} %fusion.45, f32[128,32,256]{2,1,0:T(8,128)} %bitcast.199), kind=kCustom, calls=%fused_computation.2 | custom fusion | flops 1048576 | bytes 12583424 | tf_op jit(solution)/shard_map/scatter-add | solution.py:88
  83.2 3.5 copy.80
  86.7 3.4 reshape.298
  90.3 1.7 collective-permute-start.11
  92.3 1.2 collective-permute-start.2
  94.2 1.6 constant_dynamic-update-slice_fusion.5
  95.8 1.5 collective-permute-done.2
  98.0 2.9 collective-permute-start.3
  101.0 7.6 %collective-permute-done.10 = bf16[32,4,2048]{2,1,0:T(4,128)(2,1)S(1)} collective-permute-done((bf16[32,4,2048]{2,1,0:T(4,128)(2,1)S(1)}, bf16[32,4,2048]{2,1,0:T(4,128)(2,1)S(1)}, u32[]{:S(2)}, u32[]{:S(2)}) %collective-permute-start.10) | collective-permute-done | bytes 524320 | tf_op jit(solution)/shard_map/ppermute | solution.py:10
  108.7 3.5 collective-permute-done.11
  112.6 1.6 copy.83
  114.5 6.2 %collective-permute-done.3 = bf16[32,8192]{1,0:T(8,128)(2,1)S(1)} collective-permute-done((bf16[32,8192]{1,0:T(8,128)(2,1)}, bf16[32,8192]{1,0:T(8,128)(2,1)S(1)}, u32[]{:S(2)}, u32[]{:S(2)}) %collective-permute-start.3) | collective-permute-done | bytes 524320 | tf_op jit(solution)/shard_map/ppermute | solution.py:10
  120.7 1.1 pad_maximum_fusion
  121.8 1.4 copy.141
  123.2 2.1 gather_fusion
  125.3 11.1 %fusion.10 = f32[8,4,8,256]{3,2,1,0:T(8,128)S(1)} fusion(bf16[32,8,16,256]{3,0,2,1:T(8,128)(2,1)S(1)} %bitcast.202, bf16[1,1,8,16,256,256]{5,4,3,2,1,0:T(8,128)(2,1)} %param.10), kind=kOutput, calls=%fused_computation.22 | convolution fusion | flops 536870912 | bytes 19136512 | tf_op jit(solution)/shard_map/rkij,brkj->bri/dot_general | solution.py:77
  136.5 0.9 broadcast.223
  138.1 1.3 collective-permute-start.5
  140.0 1.1 collective-permute-start.6
  141.1 3.8 %collective-permute-done.5 = bf16[32,2048]{1,0:T(8,128)(2,1)S(1)} collective-permute-done((bf16[32,2048]{1,0:T(8,128)(2,1)}, bf16[32,2048]{1,0:T(8,128)(2,1)S(1)}, u32[]{:S(2)}, u32[]{:S(2)}) %collective-permute-start.5) | collective-permute-done | bytes 131104 | tf_op jit(solution)/shard_map/ppermute | solution.py:54
  144.9 1.0 copy.115
  145.9 10.6 %fusion = f32[8,32,16,256]{3,1,2,0:T(8,128)} fusion(bf16[1,1,8,16,256,256]{5,4,3,2,1,0:T(8,128)(2,1)} %param.10, bf16[32,8,256,1]{2,1,0,3:T(8,128)(2,1)S(1)} %bitcast.217), kind=kOutput, calls=%fused_computation.8 | convolution fusion | flops 536870912 | bytes 21102592 | tf_op jit(solution)/shard_map/rkij,bri->brkj/dot_general | solution.py:81
  157.2 13.5 %scatter_fusion.1 = f32[32,96,256]{2,0,1:T(8,128)S(1)} fusion(f32[32,96,256]{2,0,1:T(8,128)S(1)} %broadcast.230, s32[128]{0:T(128)S(1)} %copy-done.12, f32[128,32,256]{2,1,0:T(8,128)} %bitcast.198), kind=kCustom, calls=%fused_computation.3 | custom fusion | flops 1048576 | bytes 12583424 | tf_op jit(solution)/shard_map/scatter-add | solution.py:88
  170.7 3.5 copy.85
  174.1 3.4 reshape.302
  177.7 3.9 %collective-permute-start.13 = (f32[32,4,2048]{2,1,0:T(4,128)S(1)}, f32[32,4,2048]{2,1,0:T(4,128)S(1)}, u32[]{:S(2)}, u32[]{:S(2)}) collective-permute-start(f32[32,4,2048]{2,1,0:T(4,128)S(1)} %get-tuple-element.19), channel_id=1, source_target_pairs={{7,0},{0,1},{1,2},{2,3},{3,4},{4,5},{5,6},{6,7},{15,8},{8,9},{9,10... | collective-permute-start | bytes 3145736 | tf_op jit(solution)/shard_map/ppermute | solution.py:10
  182.6 1.6 constant_dynamic-update-slice_fusion.1
  184.2 1.6 constant_dynamic-update-slice_fusion
  185.8 1.7 collective-permute-start.8
  187.5 1.4 collective-permute-start.9
  189.0 8.7 %collective-permute-done.12 = bf16[32,4,2048]{2,1,0:T(4,128)(2,1)S(1)} collective-permute-done((bf16[32,4,2048]{2,1,0:T(4,128)(2,1)S(1)}, bf16[32,4,2048]{2,1,0:T(4,128)(2,1)S(1)}, u32[]{:S(2)}, u32[]{:S(2)}) %collective-permute-start.12) | collective-permute-done | bytes 524320 | tf_op jit(solution)/shard_map/ppermute | solution.py:10
  197.6 3.3 collective-permute-done.13
  201.4 1.6 copy.88
  203.0 7.3 %collective-permute-done.8 = bf16[32,8192]{1,0:T(8,128)(2,1)S(1)} collective-permute-done((bf16[32,8192]{1,0:T(8,128)(2,1)}, bf16[32,8192]{1,0:T(8,128)(2,1)S(1)}, u32[]{:S(2)}, u32[]{:S(2)}) %collective-permute-start.8) | collective-permute-done | bytes 524320 | tf_op jit(solution)/shard_map/ppermute | solution.py:10
  210.3 1.1 pad_maximum_fusion.1
  211.5 1.4 copy.140
  212.8 2.1 gather_fusion.1
  215.0 11.1 %fusion.4 = f32[8,32,256,1]{2,1,3,0:T(8,128)S(1)} fusion(bf16[32,8,16,256]{3,0,2,1:T(8,128)(2,1)S(1)} %bitcast.201, bf16[1,1,8,16,256,256]{5,4,3,2,1,0:T(8,128)(2,1)} %param.10), kind=kOutput, calls=%fused_computation.12 | convolution fusion | flops 536870912 | bytes 19136512 | tf_op jit(solution)/shard_map/rkij,brkj->bri/dot_general | solution.py:77
  226.2 8.6 %reduce-scatter.9.cloned.1.call-done = f32[32,1,2048]{2,0,1:T(8,128)} async-done(((f32[32,4,2048]{2,0,1:T(8,128)}), f32[32,1,2048]{2,0,1:T(8,128)}) %reduce-scatter.9.cloned.1.call-update) | async-done | bytes 262160
  234.8 1.1 fusion.29
  235.9 1.3 copy.90
  237.2 6.7 %scatter_custom_fusion.5 = f32[32,6144]{0,1:T(8,128)S(1)} fusion(s32[2048]{0:T(1024)} %broadcast_select_fusion, f32[2048,32]{1,0:T(8,128)} %copy.90, f32[]{:T(128)} %constant.93.clone.1), kind=kCustom, calls=%fused_computation.20 | custom fusion | bytes 786944
  244.0 2.2 copy.91
  246.2 5.0 %all-to-all-start.4 = ((f32[32,32,192]{2,0,1:T(8,128)}), f32[32,32,192]{2,0,1:T(8,128)S(1)}, u32[]{:S(2)}, u32[]{:S(2)}) async-start(f32[32,32,192]{2,0,1:T(8,128)} %copy.91), calls=%async_computation.4 | async-start | bytes 2097152 | tf_op jit(solution)/shard_map/all_to_all | solution.py:131
  251.2 0.8 reduce.4
  252.1 42.6 %scatter_custom_fusion.3 = f32[1025]{0:T(1024)S(1)} fusion(s32[6144]{0:T(1024)S(1)} %reshape.348, f32[6144]{0:T(1024)S(1)} %broadcast.249, f32[]{:T(128)} %constant.93.clone.1), kind=kCustom, calls=%fused_computation.87 | custom fusion | flops 6144 | bytes 4104 | tf_op jit(solution)/shard_map/scatter-add | solution.py:139
  294.8 1.1 copy.76
  296.0 1.0 copy.94
  297.6 1.3 reshape.305
  298.9 2.0 copy.93
  300.9 41.4 %scatter_custom_fusion.2 = f32[1025,32]{1,0:T(8,128)} fusion(s32[6144]{0:T(1024)S(1)} %reshape.348, f32[6144,32]{1,0:T(8,128)S(1)} %copy.93, f32[]{:T(128)} %constant.93.clone.1), kind=kCustom, calls=%fused_computation.37 | custom fusion | flops 196608 | bytes 131204 | tf_op jit(solution)/shard_map/scatter-add | solution.py:136
  342.3 1.2 fusion.19
  343.5 0.8 copy.95
  (100 shorter events, 13.5 us)
Async XLA Ops:
  7.2 16.7 %copy-start.16 = (s32[2]{0:T(128)S(1)}, s32[2]{0:T(128)}, u32[]{:S(2)}) copy-start(s32[2]{0:T(128)} %constant.106) | copy-start | bytes 28
  7.2 16.8 %copy-start.13 = (s32[3]{0:T(128)S(1)}, s32[3]{0:T(128)}, u32[]{:S(2)}) copy-start(s32[3]{0:T(128)} %constant.100) | copy-start | bytes 40
  7.2 16.9 %copy-start.15 = (s32[3]{0:T(128)S(1)}, s32[3]{0:T(128)}, u32[]{:S(2)}) copy-start(s32[3]{0:T(128)} %constant.103) | copy-start | bytes 40
  7.2 26.0 %copy-start.14 = (s32[2]{0:T(128)S(1)}, s32[2]{0:T(128)}, u32[]{:S(2)}) copy-start(s32[2]{0:T(128)} %constant.109) | copy-start | bytes 28
  7.2 16.6 %copy-start.11 = (s32[1,1,2048,1]{2,3,1,0:T(1,128)S(1)}, s32[1,1,2048,1]{2,3,1,0:T(1,128)}, u32[]{:S(2)}) copy-start(s32[1,1,2048,1]{2,3,1,0:T(1,128)} %param.12) | copy-start | bytes 24580
  7.2 26.1 %all-to-all-start = ((f32[8,4,2048]{2,0,1:T(8,128)}), f32[8,4,2048]{2,0,1:T(8,128)S(1)}, u32[]{:S(2)}, u32[]{:S(2)}) async-start(f32[8,4,2048]{2,0,1:T(8,128)} %bitcast.219), calls=%async_computation | async-start | bytes 524288 | tf_op jit(solution)/shard_map/all_to_all | solution.py:17
  33.3 7.9 %all-to-all-start.1 = ((f32[8,4,2048]{2,0,1:T(8,128)}), f32[8,4,2048]{2,0,1:T(8,128)S(1)}, u32[]{:S(2)}, u32[]{:S(2)}) async-start(f32[8,4,2048]{2,0,1:T(8,128)} %bitcast.2), calls=%async_computation.1 | async-start | bytes 524288 | tf_op jit(solution)/shard_map/all_to_all | solution.py:18
  41.2 28.1 %copy-start = (f32[8,4,2048]{2,0,1:T(8,128)}, f32[8,4,2048]{2,0,1:T(8,128)S(1)}, u32[]{:S(2)}) copy-start(f32[8,4,2048]{2,0,1:T(8,128)S(1)} %all-to-all-done.1) | copy-start | bytes 786436
  41.2 7.6 %all-to-all-start.3 = ((f32[8,4,2048]{2,0,1:T(8,128)}), f32[8,4,2048]{2,0,1:T(8,128)S(1)}, u32[]{:S(2)}, u32[]{:S(2)}) async-start(f32[8,4,2048]{2,0,1:T(8,128)} %bitcast.30), calls=%async_computation.3 | async-start | bytes 524288 | tf_op jit(solution)/shard_map/all_to_all | solution.py:19
  46.2 46.1 %collective-permute-start = (bf16[32,2048]{1,0:T(8,128)(2,1)}, bf16[32,2048]{1,0:T(8,128)(2,1)S(1)}, u32[]{:S(2)}, u32[]{:S(2)}) collective-permute-start(bf16[32,2048]{1,0:T(8,128)(2,1)} %get-tuple-element.17), channel_id=1, source_target_pairs={{0,8},{8,16},{16,24},{24,0},{1,9},{9,17},{17,25},{25,1},{2,10},{10... | collective-permute-start | bytes 393224 | tf_op jit(solution)/shard_map/ppermute | solution.py:54
  47.6 46.6 %collective-permute-start.1 = (bf16[32,2048]{1,0:T(8,128)(2,1)}, bf16[32,2048]{1,0:T(8,128)(2,1)}, u32[]{:S(2)}, u32[]{:S(2)}) collective-permute-start(bf16[32,2048]{1,0:T(8,128)(2,1)} %get-tuple-element.17), channel_id=1, source_target_pairs={{0,24},{8,0},{16,8},{24,16},{1,25},{9,1},{17,9},{25,17},{2,26},{10... | collective-permute-start | bytes 393224 | tf_op jit(solution)/shard_map/ppermute | solution.py:62
  48.6 20.6 %copy-start.7 = (f32[4,8,8,256]{3,2,1,0:T(8,128)}, f32[4,8,8,256]{3,2,1,0:T(8,128)S(1)}, u32[]{:S(2)}) copy-start(f32[4,8,8,256]{3,2,1,0:T(8,128)S(1)} %copy.113) | copy-start | bytes 786436
  48.8 20.5 %copy-start.5 = (f32[8,4,2048]{2,0,1:T(8,128)}, f32[8,4,2048]{2,0,1:T(8,128)S(1)}, u32[]{:S(2)}) copy-start(f32[8,4,2048]{2,0,1:T(8,128)S(1)} %all-to-all-done.3) | copy-start | bytes 786436
  48.8 197.4 %all-to-all-start.2 = ((s32[1,32,192]{2,0,1:T(1,128)}), s32[1,32,192]{2,0,1:T(1,128)}, u32[]{:S(2)}, u32[]{:S(2)}) async-start(s32[1,32,192]{2,0,1:T(1,128)} %reshape.309), calls=%async_computation.2 | async-start | bytes 65536 | tf_op jit(solution)/shard_map/all_to_all | solution.py:132
  58.5 86.4 %reduce-scatter.7.cloned.1.call-start = ((), (), s32[]{:S(2)}) async-start(), calls=%async_computation.7 | async-start | bytes 1310720
  90.3 21.9 %collective-permute-start.11 = (f32[32,4,2048]{2,1,0:T(4,128)S(1)}, f32[32,4,2048]{2,1,0:T(4,128)S(1)}, u32[]{:S(2)}, u32[]{:S(2)}) collective-permute-start(f32[32,4,2048]{2,1,0:T(4,128)S(1)} %get-tuple-element.21), channel_id=1, source_target_pairs={{7,0},{0,1},{1,2},{2,3},{3,4},{4,5},{5,6},{6,7},{15,8},{8,9},{9,10... | collective-permute-start | bytes 3145736 | tf_op jit(solution)/shard_map/ppermute | solution.py:10
  92.2 16.5 %collective-permute-start.10 = (bf16[32,4,2048]{2,1,0:T(4,128)(2,1)S(1)}, bf16[32,4,2048]{2,1,0:T(4,128)(2,1)S(1)}, u32[]{:S(2)}, u32[]{:S(2)}) collective-permute-start(bf16[32,4,2048]{2,1,0:T(4,128)(2,1)S(1)} %fusion.17), channel_id=1, source_target_pairs={{1,0},{2,1},{3,2},{4,3},{5,4},{6,5},{7,6},{0,7},{9,8},{10,9},{11,1... | collective-permute-start | bytes 1572872 | tf_op jit(solution)/shard_map/ppermute | solution.py:10
  92.3 5.1 %collective-permute-start.2 = (bf16[32,2048]{1,0:T(8,128)(2,1)S(1)}, bf16[32,2048]{1,0:T(8,128)(2,1)S(1)}, u32[]{:S(2)}, u32[]{:S(2)}) collective-permute-start(bf16[32,2048]{1,0:T(8,128)(2,1)S(1)} %collective-permute-done), channel_id=1, source_target_pairs={{0,8},{8,16},{16,24},{24,0},{1,9},{9,17},{17,25},{25,1},{2,10},{10... | collective-permute-start | bytes 393224 | tf_op jit(solution)/shard_map/ppermute | solution.py:54
  98.0 22.6 %collective-permute-start.3 = (bf16[32,8192]{1,0:T(8,128)(2,1)}, bf16[32,8192]{1,0:T(8,128)(2,1)S(1)}, u32[]{:S(2)}, u32[]{:S(2)}) collective-permute-start(bf16[32,8192]{1,0:T(8,128)(2,1)} %constant_dynamic-update-slice_fusion.4), channel_id=1, source_target_pairs={{7,0},{0,1},{1,2},{2,3},{3,4},{4,5},{5,6},{6,7},{15,8},{8,9},{9,10... | collective-permute-start | bytes 1572872 | tf_op jit(solution)/shard_map/ppermute | solution.py:10
  100.9 19.8 %collective-permute-start.4 = (bf16[32,8192]{1,0:T(8,128)(2,1)}, bf16[32,8192]{1,0:T(8,128)(2,1)S(1)}, u32[]{:S(2)}, u32[]{:S(2)}) collective-permute-start(bf16[32,8192]{1,0:T(8,128)(2,1)} %constant_dynamic-update-slice_fusion.4), channel_id=1, source_target_pairs={{1,0},{2,1},{3,2},{4,3},{5,4},{6,5},{7,6},{0,7},{9,8},{10,9},{11,1... | collective-permute-start | bytes 1572872 | tf_op jit(solution)/shard_map/ppermute | solution.py:10
  114.3 120.5 %reduce-scatter.9.cloned.1.call-start = ((), (), s32[]{:S(2)}) async-start(), calls=%async_computation.8 | async-start | bytes 1310720
  125.3 12.1 %copy-start.1 = (f32[8,4,2048]{2,0,1:T(8,128)S(1)}, f32[8,4,2048]{2,0,1:T(8,128)}, u32[]{:S(2)}) copy-start(f32[8,4,2048]{2,0,1:T(8,128)} %copy-done) | copy-start | bytes 786436
  125.3 20.6 %copy-start.8 = (f32[4,8,8,256]{3,2,1,0:T(8,128)S(1)}, f32[4,8,8,256]{3,2,1,0:T(8,128)}, u32[]{:S(2)}) copy-start(f32[4,8,8,256]{3,2,1,0:T(8,128)} %copy-done.7) | copy-start | bytes 786436
  136.5 20.1 %copy-start.9 = (f32[8,4,8,256]{3,2,0,1:T(8,128)}, f32[8,4,8,256]{3,2,0,1:T(8,128)S(1)}, u32[]{:S(2)}) copy-start(f32[8,4,8,256]{3,2,0,1:T(8,128)S(1)} %copy.111) | copy-start | bytes 786436
  138.1 6.8 %collective-permute-start.5 = (bf16[32,2048]{1,0:T(8,128)(2,1)}, bf16[32,2048]{1,0:T(8,128)(2,1)S(1)}, u32[]{:S(2)}, u32[]{:S(2)}) collective-permute-start(bf16[32,2048]{1,0:T(8,128)(2,1)} %get-tuple-element.13), channel_id=1, source_target_pairs={{0,8},{8,16},{16,24},{24,0},{1,9},{9,17},{17,25},{25,1},{2,10},{10... | collective-permute-start | bytes 393224 | tf_op jit(solution)/shard_map/ppermute | solution.py:54
  140.0 42.7 %collective-permute-start.6 = (bf16[32,2048]{1,0:T(8,128)(2,1)}, bf16[32,2048]{1,0:T(8,128)(2,1)}, u32[]{:S(2)}, u32[]{:S(2)}) collective-permute-start(bf16[32,2048]{1,0:T(8,128)(2,1)} %get-tuple-element.13), channel_id=1, source_target_pairs={{0,24},{8,0},{16,8},{24,16},{1,25},{9,1},{17,9},{25,17},{2,26},{10... | collective-permute-start | bytes 393224 | tf_op jit(solution)/shard_map/ppermute | solution.py:62
  144.9 39.3 %collective-permute-start.7 = (bf16[32,2048]{1,0:T(8,128)(2,1)S(1)}, bf16[32,2048]{1,0:T(8,128)(2,1)}, u32[]{:S(2)}, u32[]{:S(2)}) collective-permute-start(bf16[32,2048]{1,0:T(8,128)(2,1)S(1)} %collective-permute-done.5), channel_id=1, source_target_pairs={{0,8},{8,16},{16,24},{24,0},{1,9},{9,17},{17,25},{25,1},{2,10},{10... | collective-permute-start | bytes 393224 | tf_op jit(solution)/shard_map/ppermute | solution.py:54
  156.6 0.6 copy-start.12
  177.7 23.2 %collective-permute-start.13 = (f32[32,4,2048]{2,1,0:T(4,128)S(1)}, f32[32,4,2048]{2,1,0:T(4,128)S(1)}, u32[]{:S(2)}, u32[]{:S(2)}) collective-permute-start(f32[32,4,2048]{2,1,0:T(4,128)S(1)} %get-tuple-element.19), channel_id=1, source_target_pairs={{7,0},{0,1},{1,2},{2,3},{3,4},{4,5},{5,6},{6,7},{15,8},{8,9},{9,10... | collective-permute-start | bytes 3145736 | tf_op jit(solution)/shard_map/ppermute | solution.py:10
  181.8 15.8 %collective-permute-start.12 = (bf16[32,4,2048]{2,1,0:T(4,128)(2,1)S(1)}, bf16[32,4,2048]{2,1,0:T(4,128)(2,1)S(1)}, u32[]{:S(2)}, u32[]{:S(2)}) collective-permute-start(bf16[32,4,2048]{2,1,0:T(4,128)(2,1)S(1)} %fusion.18), channel_id=1, source_target_pairs={{1,0},{2,1},{3,2},{4,3},{5,4},{6,5},{7,6},{0,7},{9,8},{10,9},{11,1... | collective-permute-start | bytes 1572872 | tf_op jit(solution)/shard_map/ppermute | solution.py:10
  185.8 24.5 %collective-permute-start.8 = (bf16[32,8192]{1,0:T(8,128)(2,1)}, bf16[32,8192]{1,0:T(8,128)(2,1)S(1)}, u32[]{:S(2)}, u32[]{:S(2)}) collective-permute-start(bf16[32,8192]{1,0:T(8,128)(2,1)} %constant_dynamic-update-slice_fusion), channel_id=1, source_target_pairs={{7,0},{0,1},{1,2},{2,3},{3,4},{4,5},{5,6},{6,7},{15,8},{8,9},{9,10... | collective-permute-start | bytes 1572872 | tf_op jit(solution)/shard_map/ppermute | solution.py:10
  187.5 22.8 %collective-permute-start.9 = (bf16[32,8192]{1,0:T(8,128)(2,1)}, bf16[32,8192]{1,0:T(8,128)(2,1)S(1)}, u32[]{:S(2)}, u32[]{:S(2)}) collective-permute-start(bf16[32,8192]{1,0:T(8,128)(2,1)} %constant_dynamic-update-slice_fusion), channel_id=1, source_target_pairs={{1,0},{2,1},{3,2},{4,3},{5,4},{6,5},{7,6},{0,7},{9,8},{10,9},{11,1... | collective-permute-start | bytes 1572872 | tf_op jit(solution)/shard_map/ppermute | solution.py:10
  215.0 19.8 %copy-start.2 = (f32[8,4,2048]{2,0,1:T(8,128)S(1)}, f32[8,4,2048]{2,0,1:T(8,128)}, u32[]{:S(2)}) copy-start(f32[8,4,2048]{2,0,1:T(8,128)} %copy-done) | copy-start | bytes 786436
  215.0 19.8 %copy-start.6 = (f32[8,4,2048]{2,0,1:T(8,128)S(1)}, f32[8,4,2048]{2,0,1:T(8,128)}, u32[]{:S(2)}) copy-start(f32[8,4,2048]{2,0,1:T(8,128)} %copy-done.5) | copy-start | bytes 786436
  215.0 19.8 %copy-start.10 = (f32[8,4,8,256]{3,2,0,1:T(8,128)S(1)}, f32[8,4,8,256]{3,2,0,1:T(8,128)}, u32[]{:S(2)}) copy-start(f32[8,4,8,256]{3,2,0,1:T(8,128)} %copy-done.9) | copy-start | bytes 786436
  226.1 9.8 %copy-start.4 = (f32[8,32,256,1]{2,1,3,0:T(8,128)}, f32[8,32,256,1]{2,1,3,0:T(8,128)S(1)}, u32[]{:S(2)}) copy-start(f32[8,32,256,1]{2,1,3,0:T(8,128)S(1)} %fusion.4) | copy-start | bytes 786436
  246.2 49.8 %copy-start.3 = (f32[8,4,2048]{2,0,1:T(8,128)S(1)}, f32[8,4,2048]{2,0,1:T(8,128)}, u32[]{:S(2)}) copy-start(f32[8,4,2048]{2,0,1:T(8,128)} %copy-done) | copy-start | bytes 786436
  246.2 50.8 %all-to-all-start.4 = ((f32[32,32,192]{2,0,1:T(8,128)}), f32[32,32,192]{2,0,1:T(8,128)S(1)}, u32[]{:S(2)}, u32[]{:S(2)}) async-start(f32[32,32,192]{2,0,1:T(8,128)} %copy.91), calls=%async_computation.4 | async-start | bytes 2097152 | tf_op jit(solution)/shard_map/all_to_all | solution.py:131
Sparse Core Ops, SparseCore 0:
  114.4 29.7 reduce-scatter.6
  203.1 31.6 reduce-scatter.8
